TPU v7x, 32 devices: a whole 2x2x4 slice. The times are simulated.
32 devices in a mesh: seq: 4 (over y, core), dp: 8 (over z, x).
Axes of the slice: x: 2, y: 2, z: 4, core: 2. Of those that a mesh axis runs over, the one named last changes fastest.
Arguments:
- mlp_hidden: bfloat16 [8, 256, 8192], P('dp', None, 'seq'), may hold values from -6 to 6
- encoder_stream: bfloat16 [8, 256, 4096], P('dp', 'seq'), may hold values from -18 to 18
- down_proj: bfloat16 [8192, 4096], P('seq', 'dp'), may hold values from -0.0625 to 0.0625
- final_gain: bfloat16 [4096], replicated, may hold values from 0.25 to 1.75
- kv_proj: bfloat16 [4096, 2, 2048], P('dp', None, 'seq'), may hold values from -0.09375 to 0.09375
- queries: bfloat16 [8, 128, 2048], P('dp', None, 'seq'), may hold values from -640 to 640
- out_proj: bfloat16 [2048, 4096], P('seq'), may hold values from -0.39648438 to 0.39648438
- enc_len: int32 [8], P('dp'), may hold values from 128 to 256, as said below
- dec_pad: int32 [8], P('dp'), may hold values from 0 to 64, as said below
Outputs:
- cross_out: bfloat16 [8, 128, 4096], P('dp', 'seq')
Inputs may be any that keep to these rules, and one draw needn't show every extreme that they name: `enc_len`: at least one filing uses all 256 positions and one uses 256 // 2. `dec_pad`: some filing has no padding and some has 64 padded rows.
All inputs are finite; a program needn't handle non-finite values.
Results may differ from a plain program's by a relative error of at most 0.015.
The roundings to bfloat16 on the way count: a program that leaves them out, or rounds other values in their place, can miss the bound.
Values may be sent and summed in bfloat16 or wider, within the bound.
No kernel may reach another device: no remote copies, remote signals or barrier semaphores. Data moves between devices by JAX's collectives and lax.ppermute only.
A program may use at most 128 MiB of HBM per device.

v0:
```python
import math
import jax
import jax.numpy as jnp
from jax import lax
from jax.sharding import PartitionSpec as P

HD = 256


def normalize(resid, gain_row):
    spread = jnp.mean(resid * resid, axis=-1, keepdims=True)
    return (resid * lax.rsqrt(spread + 1e-06) * gain_row).astype(jnp.bfloat16)


def on_device(
    mlp_hidden, encoder_stream, down_proj, final_gain, kv_proj, queries, out_proj, enc_len, dec_pad
):
    hidden = mlp_hidden[0]
    enc_total = hidden.shape[0]
    gain_row = final_gain.astype(jnp.float32)
    full_down = lax.all_gather(down_proj, "dp", axis=1, tiled=True)
    row_block = hidden
    mlp_out = lax.psum_scatter(
        jnp.dot(row_block, full_down, preferred_element_type=jnp.float32),
        "seq",
        scatter_dimension=0,
        tiled=True,
    )
    normed = normalize(encoder_stream[0].astype(jnp.float32) + mlp_out, gain_row)
    encoded = lax.all_gather(normed, "seq", axis=0, tiled=True)
    heads_here = queries.shape[2] // HD
    kv_width = 2 * heads_here * HD
    weight_piece = lax.all_gather(kv_proj, "dp", axis=0, tiled=True)
    key_value = jnp.dot(
        encoded,
        weight_piece.reshape(weight_piece.shape[0], kv_width),
        preferred_element_type=jnp.float32,
    ).astype(jnp.bfloat16)
    key_value = key_value.reshape(enc_total, 2, heads_here, HD)
    key_rows = key_value[:, 0]
    value_rows = key_value[:, 1]
    dec_rows = queries.shape[1]
    query_rows = queries[0].reshape(dec_rows, heads_here, HD)
    scores = jnp.einsum(
        "qhd,khd->hqk", query_rows, key_rows, preferred_element_type=jnp.float32
    ) / math.sqrt(HD)
    visible = jnp.arange(enc_total, dtype=jnp.int32) < enc_len[0]
    scores = jnp.where(visible[None, None, :], scores, -jnp.inf)
    highest = jnp.max(scores, axis=-1, keepdims=True)
    expo = jnp.exp(scores - highest)
    attention = (expo / jnp.sum(expo, axis=-1, keepdims=True)).astype(jnp.bfloat16)
    attended = jnp.einsum(
        "hqk,khd->qhd", attention, value_rows, preferred_element_type=jnp.float32
    ).astype(jnp.bfloat16)
    row_live = jnp.arange(dec_rows, dtype=jnp.int32) < dec_rows - dec_pad[0]
    attended = jnp.where(row_live[:, None, None], attended, jnp.zeros_like(attended)).reshape(
        dec_rows, heads_here * HD
    )
    row_block = attended
    result = lax.psum_scatter(
        jnp.dot(row_block, out_proj, preferred_element_type=jnp.float32),
        "seq",
        scatter_dimension=0,
        tiled=True,
    )
    return result.astype(jnp.bfloat16)[None]


def solution(mesh):
    placed = (
        P("dp", None, "seq"),
        P("dp", "seq", None),
        P("seq", "dp"),
        P(),
        P("dp", None, "seq"),
        P("dp", None, "seq"),
        P("seq", None),
        P("dp"),
        P("dp"),
    )
    return jax.shard_map(
        on_device, mesh=mesh, in_specs=placed, out_specs=P("dp", "seq", None), check_vma=False
    )
```

profile of v0, /device:TPU:0, one launch (start us, length us, event | category | flops | bytes accessed | tf_op | source)
XLA Modules:
  0.0 494.5 jit_solution(16718448679306863005)
XLA Ops:
  6.5 0.0 copy-start
  6.5 0.0 all-gather.4.cloned.1.call-start
  6.5 0.7 all-gather.4.cloned.1.call-update
  7.3 0.0 reduce-scatter.3.cloned.1.call-start
  7.3 232.6 %all-gather.4.cloned.1.call-done = bf16[2048,4096]{1,0:T(8,128)(2,1)} async-done(((bf16[2048,512]{1,0:T(8,128)(2,1)}), bf16[2048,4096]{1,0:T(8,128)(2,1)}) %all-gather.4.cloned.1.call-update) | async-done | bytes 16777232 | tf_op jit(solution)/shard_map/all_gather | solution.py:21
  239.9 0.0 copy-done
  239.9 10.1 %fusion.6 = f32[256,4096]{1,0:T(8,128)} fusion(bf16[2048,4096]{1,0:T(8,128)(2,1)} %all-gather.4.cloned.1.call-done, bf16[1,256,2048]{2,1,0:T(8,128)(2,1)S(1)} %copy-done), kind=kOutput, calls=%fused_computation.10 | convolution fusion | flops 4294967296 | bytes 22020096 | tf_op jit(solution)/shard_map/dot_general | solution.py:24
  250.0 0.0 copy-start.3
  250.0 0.0 copy-start.1
  250.0 0.0 copy-start.2
  250.0 0.0 reduce-scatter.3.cloned.1.call-update
  250.0 0.0 all-gather.8.cloned.1.call-start
  250.0 0.7 all-gather.8.cloned.1.call-update
  250.7 0.0 all-gather.6.cloned.1.call-start
  250.8 0.0 copy-done.3
  250.8 42.0 %reduce-scatter.3.cloned.1.call-done = f32[64,4096]{1,0:T(8,128)} async-done(((f32[256,4096]{1,0:T(8,128)}), f32[64,4096]{1,0:T(8,128)}) %reduce-scatter.3.cloned.1.call-update) | async-done | bytes 1048592 | tf_op jit(solution)/shard_map/reduce_scatter | solution.py:23
  292.8 0.0 copy-done.1
  292.8 1.5 multiply_reduce_fusion
  294.3 2.2 multiply_convert_fusion
  296.5 0.0 all-gather.6.cloned.1.call-update
  296.5 0.0 reduce-scatter.5.cloned.1.call-start
  296.6 0.0 copy-done.2
  297.9 122.2 %all-gather.8.cloned.1.call-done = bf16[4096,2,512]{2,1,0:T(2,128)(2,1)} async-done(((bf16[512,2,512]{2,1,0:T(2,128)(2,1)}), bf16[4096,2,512]{2,1,0:T(2,128)(2,1)}) %all-gather.8.cloned.1.call-update) | async-done | bytes 8388624 | tf_op jit(solution)/shard_map/all_gather | solution.py:33
  420.1 9.3 %copy.21 = bf16[512,8,2,512]{3,1,2,0:T(8,128)(2,1)} copy(bf16[512,8,2,512]{3,2,1,0:T(2,128)(2,1)} %bitcast.32) | data formatting | bytes 16777216
  429.4 13.0 %all-gather.6.cloned.1.call-done = bf16[256,4096]{1,0:T(8,128)(2,1)} async-done(((bf16[64,4096]{1,0:T(8,128)(2,1)}), bf16[256,4096]{1,0:T(8,128)(2,1)}) %all-gather.6.cloned.1.call-update) | async-done | bytes 2097168 | tf_op jit(solution)/shard_map/all_gather | solution.py:30
  442.4 6.3 %convolution_convert_fusion = bf16[256,1024]{1,0:T(8,128)(2,1)S(1)} fusion(bf16[256,4096]{1,0:T(8,128)(2,1)} %all-gather.6.cloned.1.call-done, bf16[4096,1024]{1,0:T(8,128)(2,1)} %bitcast.33), kind=kOutput, calls=%fused_computation.1 | convolution fusion | flops 2147745792 | bytes 11010048 | tf_op jit(solution)/shard_map/dot_general | solution.py:34
  448.8 0.4 reshape.33
  449.2 0.4 fusion.12
  449.5 0.2 fusion.3
  449.8 0.1 fusion.13
  449.9 0.2 copy.19
  450.1 0.3 fusion.5
  450.3 4.3 fusion.14
  454.6 0.0 reduce-scatter.5.cloned.1.call-update
  454.6 31.6 %reduce-scatter.5.cloned.1.call-done = f32[32,4096]{1,0:T(8,128)} async-done(((f32[128,4096]{1,0:T(8,128)}), f32[32,4096]{1,0:T(8,128)}) %reduce-scatter.5.cloned.1.call-update) | async-done | bytes 524304 | tf_op jit(solution)/shard_map/reduce_scatter | solution.py:60
  486.2 1.8 convert_bitcast_fusion
  (5 shorter events, 0.1 us)
Async XLA Ops:
  6.5 233.4 %copy-start = (bf16[1,256,2048]{2,1,0:T(8,128)(2,1)S(1)}, bf16[1,256,2048]{2,1,0:T(8,128)(2,1)}, u32[]{:S(2)}) copy-start(bf16[1,256,2048]{2,1,0:T(8,128)(2,1)} %param.9) | copy-start | bytes 3145732
  6.5 233.3 %all-gather.4.cloned.1.call-start = ((), (), s32[]{:S(2)}) async-start(), calls=%async_computation.2 | async-start | bytes 18874368 | tf_op jit(solution)/shard_map/all_gather | solution.py:21
  7.3 285.6 %reduce-scatter.3.cloned.1.call-start = ((), (), s32[]{:S(2)}) async-start(), calls=%async_computation.3 | async-start | bytes 5242880 | tf_op jit(solution)/shard_map/reduce_scatter | solution.py:23
  250.0 0.8 copy-start.3
  250.0 42.9 %copy-start.1 = (bf16[1,64,4096]{2,1,0:T(8,128)(2,1)S(1)}, bf16[1,64,4096]{2,1,0:T(8,128)(2,1)}, u32[]{:S(2)}) copy-start(bf16[1,64,4096]{2,1,0:T(8,128)(2,1)} %param.10) | copy-start | bytes 1572868
  250.0 46.6 %copy-start.2 = (bf16[1,128,512]{2,1,0:T(8,128)(2,1)S(1)}, bf16[1,128,512]{2,1,0:T(8,128)(2,1)}, u32[]{:S(2)}) copy-start(bf16[1,128,512]{2,1,0:T(8,128)(2,1)} %param.14) | copy-start | bytes 393220
  250.0 170.1 %all-gather.8.cloned.1.call-start = ((), (), s32[]{:S(2)}) async-start(), calls=%async_computation.5 | async-start | bytes 9437184 | tf_op jit(solution)/shard_map/all_gather | solution.py:33
  250.7 191.7 %all-gather.6.cloned.1.call-start = ((), (), s32[]{:S(2)}) async-start(), calls=%async_computation.4 | async-start | bytes 2621440 | tf_op jit(solution)/shard_map/all_gather | solution.py:30
  296.5 189.7 %reduce-scatter.5.cloned.1.call-start = ((), (), s32[]{:S(2)}) async-start(), calls=%async_computation.6 | async-start | bytes 2621440 | tf_op jit(solution)/shard_map/reduce_scatter | solution.py:60
Sparse Core Ops, SparseCore 0:
  9.4 230.4 all-gather.3
  250.1 42.6 reduce-scatter.2
  295.2 124.9 all-gather.7
  421.6 20.7 all-gather.5
  454.8 31.3 reduce-scatter.4
where the time goes:
time: 495 us
  waiting for transfers between devices  443 us (89%)
  matrix products  21.2 us (4%)
  between operations  14.5 us (3%)
  local copies, waits for them, and re-layouts  10.3 us (2%)
  other arithmetic  5.56 us (1%)
    all_gather x1, waiting for transfers between devices, on_device(): full_down = lax.all_gather(down_proj, 'dp', axis=1, tiled=True)  233 us
    all_gather x1, waiting for transfers between devices, on_device(): weight_piece = lax.all_gather(kv_proj, 'dp', axis=0, tiled=True)  122 us
    reduce_scatter x1, waiting for transfers between devices, on_device(): lax.psum_scatter(jnp.dot(row_block, full_down, preferred_element_type=jnp...  42 us
    reduce_scatter x1, waiting for transfers between devices, on_device(): lax.psum_scatter(jnp.dot(row_block, out_proj, preferred_element_type=jnp....  31.6 us
    all_gather x1, waiting for transfers between devices, on_device(): encoded = lax.all_gather(normed, 'seq', axis=0, tiled=True)  13 us
    dot_general x1, matrix products, on_device(): jnp.dot(row_block, full_down, preferred_element_type=jnp.float32)  10.1 us
  transfers between devices with their start and end apart: 5, of which 5 were waited for; matrix products, arithmetic and copies ran while one was open for 3% of the time, Pallas kernels for 0%

commit v1 on v0

--- a/solution.py
+++ b/solution.py
@@ -18,7 +18,14 @@
     hidden = mlp_hidden[0]
     enc_total = hidden.shape[0]
     gain_row = final_gain.astype(jnp.float32)
-    full_down = lax.all_gather(down_proj, "dp", axis=1, tiled=True)
+    ways, here = (lax.axis_size("dp"), lax.axis_index("dp"))
+    full_down, reach = (down_proj, 1)
+    while reach < ways:
+        theirs = lax.ppermute(full_down, "dp", [(d, d ^ reach) for d in range(ways)])
+        mine_first = jnp.concatenate([full_down, theirs], axis=1)
+        theirs_first = jnp.concatenate([theirs, full_down], axis=1)
+        full_down = jnp.where(here & reach == 0, mine_first, theirs_first)
+        reach = 2 * reach
     row_block = hidden
     mlp_out = lax.psum_scatter(
         jnp.dot(row_block, full_down, preferred_element_type=jnp.float32),

time: 495 us -> 755 us (1.53)
  waiting for transfers between devices: 443 us -> 659 us
  other arithmetic: 5.56 us -> 20.1 us
  local copies, waits for them, and re-layouts: 10.3 us -> 20.6 us
  matrix products: 21.2 us -> 31.1 us
    ppermute x0 -> x3, waiting for transfers between devices: none -> 495 us  [on_device(): lax.ppermute(full_down, 'dp', [(d, d ^ reach) for d in range(ways)])]
    all_gather x1 -> x0, waiting for transfers between devices: 233 us -> none  [on_device(): full_down = lax.all_gather(down_proj, 'dp', axis=1, tiled=True)]
    all_gather x1, waiting for transfers between devices: 122 us -> 74.7 us  [on_device(): weight_piece = lax.all_gather(kv_proj, 'dp', axis=0, tiled=True)]
    unnamed x5, waiting for transfers between devices: 1.44 us -> 44.9 us
    reduce_scatter x1 -> x0, waiting for transfers between devices: 42 us -> none  [on_device(): lax.psum_scatter(jnp.dot(row_block, full_down, preferred_element_type=jnp...]
    select_n x0 -> x2, other arithmetic: none -> 16.1 us  [on_device(): full_down = jnp.where(here & reach == 0, mine_first, theirs_first)]
    dot_general x1, matrix products: 10.1 us -> 19.9 us  [on_device(): jnp.dot(row_block, full_down, preferred_element_type=jnp.float32)]
    unnamed x10 -> x15, local copies, waits for them, and re-layouts: 9.51 us -> 17.5 us
  transfers between devices with their start and end apart: 5 -> 7, of which waited for: 5 -> 7; matrix products, arithmetic and copies ran while one was open for 3% -> 2% of each run, Pallas kernels for 0% -> 0%
where the time goes in v1:
time: 755 us
  waiting for transfers between devices  659 us (87%)
  matrix products  31.1 us (4%)
  local copies, waits for them, and re-layouts  20.6 us (3%)
  other arithmetic  20.1 us (3%)
  between operations  16.3 us (2%)
  starting transfers between devices  7.6 us (1%)
    ppermute x3, waiting for transfers between devices, on_device(): lax.ppermute(full_down, 'dp', [(d, d ^ reach) for d in range(ways)])  495 us
    all_gather x1, waiting for transfers between devices, on_device(): weight_piece = lax.all_gather(kv_proj, 'dp', axis=0, tiled=True)  74.7 us
    unnamed x5, waiting for transfers between devices  44.9 us
    reduce_scatter x1, waiting for transfers between devices, on_device(): lax.psum_scatter(jnp.dot(row_block, out_proj, preferred_element_type=jnp....  31.6 us
    dot_general x1, matrix products, on_device(): jnp.dot(row_block, full_down, preferred_element_type=jnp.float32)  19.9 us
    unnamed x15, local copies, waits for them, and re-layouts  17.5 us
    select_n x2, other arithmetic, on_device(): full_down = jnp.where(here & reach == 0, mine_first, theirs_first)  16.1 us
  transfers between devices with their start and end apart: 7, of which 7 were waited for; matrix products, arithmetic and copies ran while one was open for 2% of the time, Pallas kernels for 0%

profile of v1, /device:TPU:0, one launch (start us, length us, event | category | flops | bytes accessed | tf_op | source)
XLA Modules:
  0.0 755.0 jit_solution(8024178769809628517)
XLA Ops:
  7.4 0.0 copy-start
  7.4 0.0 reduce-scatter.7.cloned.1.call-start
  7.4 2.9 collective-permute-start
  10.3 45.8 %collective-permute-done = bf16[2048,512]{1,0:T(8,128)(2,1)S(1)} collective-permute-done((bf16[2048,512]{1,0:T(8,128)(2,1)}, bf16[2048,512]{1,0:T(8,128)(2,1)S(1)}, u32[]{:S(2)}, u32[]{:S(2)}) %collective-permute-start) | collective-permute-done | bytes 2097184 | tf_op jit(solution)/shard_map/ppermute | solution.py:24
  56.1 4.9 maximum_select_fusion.5
  61.0 1.8 collective-permute-start.1
  62.8 90.2 %collective-permute-done.1 = bf16[2048,1024]{1,0:T(8,128)(2,1)} collective-permute-done((bf16[2048,1024]{1,0:T(8,128)(2,1)}, bf16[2048,1024]{1,0:T(8,128)(2,1)}, u32[]{:S(2)}, u32[]{:S(2)}) %collective-permute-start.1) | collective-permute-done | bytes 4194336 | tf_op jit(solution)/shard_map/ppermute | solution.py:24
  153.1 11.2 %maximum_select_fusion.2 = bf16[2048,2048]{1,0:T(8,128)(2,1)} fusion(bf16[2048,1024]{1,0:T(8,128)(2,1)} %collective-permute-done.1, bf16[2048,1024]{1,0:T(8,128)(2,1)} %maximum_select_fusion.5, pred[]{:T(512)S(6)} %eq.10), kind=kLoop, calls=%fused_computation.9 | loop fusion | flops 37748736 | bytes 16777216 | tf_op jit(solution)/shard_map/jit(_where)/select_n | solution.py:27
  164.3 2.5 collective-permute-start.2
  166.8 359.2 %collective-permute-done.2 = bf16[2048,2048]{1,0:T(8,128)(2,1)} collective-permute-done((bf16[2048,2048]{1,0:T(8,128)(2,1)}, bf16[2048,2048]{1,0:T(8,128)(2,1)}, u32[]{:S(2)}, u32[]{:S(2)}) %collective-permute-start.2) | collective-permute-done | bytes 8388640 | tf_op jit(solution)/shard_map/ppermute | solution.py:24
  526.0 0.0 copy-done
  526.0 19.9 %fusion.8 = f32[256,4096]{0,1:T(8,128)} fusion(bf16[2048,2048]{1,0:T(8,128)(2,1)} %collective-permute-done.2, bf16[2048,2048]{1,0:T(8,128)(2,1)} %maximum_select_fusion.2, pred[]{:T(512)S(6)} %eq.9, bf16[1,256,2048]{2,1,0:T(8,128)(2,1)S(1)} %copy-done), kind=kOutput, calls=%fused_computation.10 | convolution fusion | flops 4370464768 | bytes 22020096 | tf_op jit(solution)/shard_map/dot_general | solution.py:31
  546.0 0.0 copy-start.2
  546.0 0.0 copy-start.4
  546.0 5.7 copy.22
  551.6 0.0 reduce-scatter.7.cloned.1.call-update
  551.7 0.0 copy-start.3
  551.7 0.0 all-gather.5.cloned.1.call-start
  551.7 0.5 all-gather.5.cloned.1.call-update
  552.2 0.0 all-gather.3.cloned.1.call-start
  552.3 0.0 copy-done.2
  552.3 0.5 copy.15
  552.8 0.0 copy-done.4
  552.8 44.3 %reduce-scatter.7.cloned.1.call-done = f32[64,4096]{1,0:T(8,128)} async-done(((f32[256,4096]{1,0:T(8,128)}), f32[64,4096]{1,0:T(8,128)}) %reduce-scatter.7.cloned.1.call-update) | async-done | bytes 1048592
  597.1 1.8 copy.23
  599.0 0.6 multiply_reduce_fusion
  599.5 1.5 multiply_convert_fusion
  601.1 2.3 copy.16
  603.4 0.0 all-gather.3.cloned.1.call-update
  603.4 0.2 reduce-scatter.5.cloned.1.call-start
  603.7 0.0 copy-done.3
  605.0 74.7 %all-gather.5.cloned.1.call-done = bf16[4096,2,512]{2,1,0:T(2,128)(2,1)} async-done(((bf16[512,2,512]{2,1,0:T(2,128)(2,1)}), bf16[4096,2,512]{2,1,0:T(2,128)(2,1)}) %all-gather.5.cloned.1.call-update) | async-done | bytes 8388624 | tf_op jit(solution)/shard_map/all_gather | solution.py:40
  679.8 9.3 %copy.26 = bf16[512,8,2,512]{3,1,2,0:T(8,128)(2,1)} copy(bf16[512,8,2,512]{3,2,1,0:T(2,128)(2,1)} %bitcast.34) | data formatting | bytes 16777216
  689.1 12.8 %all-gather.3.cloned.1.call-done = bf16[256,4096]{1,0:T(8,128)(2,1)} async-done(((bf16[64,4096]{1,0:T(8,128)(2,1)}), bf16[256,4096]{1,0:T(8,128)(2,1)}) %all-gather.3.cloned.1.call-update) | async-done | bytes 2097168 | tf_op jit(solution)/shard_map/all_gather | solution.py:37
  701.9 0.0 copy-start.1
  701.9 6.4 convolution_convert_fusion
  708.4 0.4 reshape.33
  708.7 0.4 fusion.20
  709.1 0.2 fusion.11
  709.4 0.1 fusion.21
  709.5 0.2 copy.24
  709.6 0.3 fusion.13
  709.9 4.3 fusion.22
  714.2 0.0 reduce-scatter.5.cloned.1.call-update
  714.2 31.6 %reduce-scatter.5.cloned.1.call-done = f32[32,4096]{1,0:T(8,128)} async-done(((f32[128,4096]{1,0:T(8,128)}), f32[32,4096]{1,0:T(8,128)}) %reduce-scatter.5.cloned.1.call-update) | async-done | bytes 524304 | tf_op jit(solution)/shard_map/reduce_scatter | solution.py:67
  745.8 1.8 convert_bitcast_fusion
  747.6 0.0 copy-done.1
  (5 shorter events, 0.1 us)
Async XLA Ops:
  7.4 518.7 %copy-start = (bf16[1,256,2048]{2,1,0:T(8,128)(2,1)S(1)}, bf16[1,256,2048]{2,1,0:T(8,128)(2,1)}, u32[]{:S(2)}) copy-start(bf16[1,256,2048]{2,1,0:T(8,128)(2,1)} %param.9) | copy-start | bytes 3145732
  7.4 589.8 %reduce-scatter.7.cloned.1.call-start = ((), (), s32[]{:S(2)}) async-start(), calls=%async_computation.5 | async-start | bytes 5242880
  7.4 48.8 %collective-permute-start = (bf16[2048,512]{1,0:T(8,128)(2,1)}, bf16[2048,512]{1,0:T(8,128)(2,1)S(1)}, u32[]{:S(2)}, u32[]{:S(2)}) collective-permute-start(bf16[2048,512]{1,0:T(8,128)(2,1)} %param.11), channel_id=1, source_target_pairs={{0,1},{1,0},{2,3},{3,2},{4,5},{5,4},{6,7},{7,6},{8,9},{9,8},{10,11... | collective-permute-start | bytes 6291464 | tf_op jit(solution)/shard_map/ppermute | solution.py:24
  61.0 92.1 %collective-permute-start.1 = (bf16[2048,1024]{1,0:T(8,128)(2,1)}, bf16[2048,1024]{1,0:T(8,128)(2,1)}, u32[]{:S(2)}, u32[]{:S(2)}) collective-permute-start(bf16[2048,1024]{1,0:T(8,128)(2,1)} %maximum_select_fusion.5), channel_id=1, source_target_pairs={{0,2},{1,3},{2,0},{3,1},{4,6},{5,7},{6,4},{7,5},{8,10},{9,11},{10,... | collective-permute-start | bytes 12582920 | tf_op jit(solution)/shard_map/ppermute | solution.py:24
  164.3 361.7 %collective-permute-start.2 = (bf16[2048,2048]{1,0:T(8,128)(2,1)}, bf16[2048,2048]{1,0:T(8,128)(2,1)}, u32[]{:S(2)}, u32[]{:S(2)}) collective-permute-start(bf16[2048,2048]{1,0:T(8,128)(2,1)} %maximum_select_fusion.2), channel_id=1, source_target_pairs={{0,4},{1,5},{2,6},{3,7},{4,0},{5,1},{6,2},{7,3},{8,12},{9,13},{10,... | collective-permute-start | bytes 25165832 | tf_op jit(solution)/shard_map/ppermute | solution.py:24
  546.0 6.3 copy-start.2
  546.0 6.8 copy-start.4
  551.7 52.0 %copy-start.3 = (bf16[1,128,512]{2,1,0:T(8,128)(2,1)S(1)}, bf16[1,128,512]{2,1,0:T(8,128)(2,1)}, u32[]{:S(2)}) copy-start(bf16[1,128,512]{2,1,0:T(8,128)(2,1)} %param.14) | copy-start | bytes 393220
  551.7 128.1 %all-gather.5.cloned.1.call-start = ((), (), s32[]{:S(2)}) async-start(), calls=%async_computation.3 | async-start | bytes 9437184 | tf_op jit(solution)/shard_map/all_gather | solution.py:40
  552.2 149.7 %all-gather.3.cloned.1.call-start = ((), (), s32[]{:S(2)}) async-start(), calls=%async_computation.2 | async-start | bytes 2621440 | tf_op jit(solution)/shard_map/all_gather | solution.py:37
  603.4 142.3 %reduce-scatter.5.cloned.1.call-start = ((), (), s32[]{:S(2)}) async-start(), calls=%async_computation.4 | async-start | bytes 2621440 | tf_op jit(solution)/shard_map/reduce_scatter | solution.py:67
  701.9 45.6 %copy-start.1 = (bf16[1,256,2048]{2,1,0:T(8,128)(2,1)S(1)}, bf16[1,256,2048]{2,1,0:T(8,128)(2,1)}, u32[]{:S(2)}) copy-start(bf16[1,256,2048]{2,1,0:T(8,128)(2,1)} %param.9) | copy-start | bytes 3145732
Sparse Core Ops, SparseCore 0:
  551.8 45.3 reduce-scatter.6
  714.3 31.3 reduce-scatter.4
Sparse Core Ops, SparseCore 1:
  554.5 125.2 all-gather.4
  681.3 20.6 all-gather.2
